TPU v7x, 256 devices: a whole 4x4x8 slice. The times are simulated.
256 devices in a mesh: tile: 32 (over z_hi, x, core), grp: 8 (over z_lo, y).
Axes of the slice: x: 4, y: 4, z: 8 (z_hi: 4, z_lo: 2; z = z_hi * 2 + z_lo), core: 2. Of those that a mesh axis runs over, the one named last changes fastest.
Arguments:
- traces: float32 [1024, 16, 1500], P(('tile', 'grp')), may hold values from -6 to 6
- validity: int32 [1024, 16], P(('tile', 'grp')), may hold values 0 or 1
- boundary_rows: int32 [256, 2, 4], P(('tile', 'grp')), may hold values from 0 to 3, as said below
- boundary_count: int32 [256, 2], P(('tile', 'grp')), may hold values from 1 to 4, as said below
- pair_mask: int32 [1024, 96], P(('tile', 'grp')), may hold values from 0 to 1, as said below
Outputs:
- correlations: bfloat16 [1024, 96, 2001], P(('tile', 'grp'))
Inputs may be any that keep to these rules, and one draw needn't show every extreme that they name: `boundary_rows`: each device's list in each direction orders all of its 4 local stations, each once. `boundary_count`: in every draw some device sends all 4 of its stations in each direction. `pair_mask`: a station's column for itself is 0.
All inputs are finite; a program needn't handle non-finite values. No bound on the sum of `validity` on one device may be relied on, other than what follows from the above.
Results may differ from a plain program's by a relative error of at most 0.008.
Values may be sent and summed in bfloat16 or wider, within the bound.
A program may use at most 64 MiB of HBM per device.

v0:
```python
import math
import jax
import jax.numpy as jnp
from jax import lax
from jax.sharding import PartitionSpec as P

SAMP = 1500
NBIN = 144
MAXLAG = 1000
LAGS = 2001


def passed_along(array, axis, by):
    count = lax.axis_size(axis)
    pairs = [(i, i + by) for i in range(count) if 0 <= i + by < count]
    return lax.ppermute(array, axis, pairs)


def fourier_table(samples):
    points = 2 * samples
    sample_number = jnp.arange(samples, dtype=jnp.int32)[:, None]
    freq_number = jnp.arange(1, NBIN + 1, dtype=jnp.int32)[None, :]
    angles = jnp.mod(sample_number * freq_number, points).astype(jnp.float32) * (
        2.0 * jnp.pi / points
    )
    return jnp.concatenate([jnp.cos(angles), -jnp.sin(angles)], axis=1)


def lag_basis():
    points = 2 * SAMP
    freq_number = jnp.arange(1, NBIN + 1, dtype=jnp.int32)[:, None]
    lag_number = jnp.arange(LAGS, dtype=jnp.int32)[None, :] - MAXLAG
    angles = jnp.mod(freq_number * lag_number, points).astype(jnp.float32) * (2.0 * jnp.pi / points)
    return jnp.concatenate([jnp.cos(angles), -jnp.sin(angles)], axis=0)


def whitened(traces, valid_float):
    stations, segments, samples = traces.shape
    sample_number = jnp.arange(samples, dtype=jnp.float32)
    hann_taper = 0.5 - 0.5 * jnp.cos(sample_number * (2.0 * jnp.pi / samples))
    flat_traces = (traces * hann_taper).reshape(stations * segments, samples)
    spectrum = jnp.dot(
        flat_traces,
        fourier_table(samples),
        precision=lax.Precision.HIGHEST,
        preferred_element_type=jnp.float32,
    )
    spectrum = spectrum.reshape(stations, segments, 2, NBIN)
    real_part = spectrum[:, :, 0]
    imag_part = spectrum[:, :, 1]
    power_bins = real_part * real_part + imag_part * imag_part
    padded = jnp.pad(power_bins, ((0, 0), (0, 0), (4, 4)))
    smooth = sum((padded[:, :, offset : offset + NBIN] for offset in range(9))) / 9.0
    mean_power = jnp.mean(power_bins, axis=2, keepdims=True)
    factor = valid_float[:, :, None] / jnp.sqrt(0.5 * smooth + 0.5 * mean_power + 1e-06)
    return jnp.stack([real_part * factor, imag_part * factor], axis=2).astype(jnp.bfloat16)


def stacked(left_spec, left_mask, right_spec, right_mask):
    left_both = jnp.concatenate([left_spec[:, :, 0], left_spec[:, :, 1]], axis=1)
    right_real = right_spec[:, :, 0]
    right_imag = right_spec[:, :, 1]
    right_both = jnp.stack(
        [
            jnp.concatenate([right_real, right_imag], axis=1),
            jnp.concatenate([-right_imag, right_real], axis=1),
        ],
        axis=1,
    )
    product = jnp.einsum(
        "iqf,jcqf->ijcf", left_both, right_both, preferred_element_type=jnp.float32
    )
    pair_count = jnp.einsum("iq,jq->ij", left_mask, right_mask, preferred_element_type=jnp.float32)
    return (product / jnp.maximum(pair_count, 1.0)[:, :, None, None]).astype(jnp.bfloat16)


def on_device(traces, validity, boundary_rows, boundary_count, pair_mask):
    per_device = traces.shape[0]
    valid_float = validity.astype(jnp.float32)
    valid_half = validity.astype(jnp.bfloat16)
    own_spec = whitened(traces, valid_float)
    slot_number = jnp.arange(per_device, dtype=jnp.int32)
    live_up = (slot_number < boundary_count[0, 0]).astype(jnp.float32)
    live_down = (slot_number < boundary_count[0, 1]).astype(jnp.float32)
    picks_up = boundary_rows[0, 0]
    picks_down = boundary_rows[0, 1]
    below_traces, below_mask = passed_along(
        (
            jnp.take(traces, picks_up, axis=0) * live_up[:, None, None],
            jnp.take(valid_float, picks_up, axis=0) * live_up[:, None],
        ),
        "tile",
        1,
    )
    above_traces, above_mask = passed_along(
        (
            jnp.take(traces, picks_down, axis=0) * live_down[:, None, None],
            jnp.take(valid_float, picks_down, axis=0) * live_down[:, None],
        ),
        "tile",
        -1,
    )
    recv_spec = whitened(
        jnp.concatenate([below_traces, above_traces], axis=0),
        jnp.concatenate([below_mask, above_mask], axis=0),
    )
    recv_mask = jnp.concatenate([below_mask, above_mask], axis=0).astype(jnp.bfloat16)
    local_spec = jnp.concatenate([own_spec, recv_spec], axis=0)
    local_mask = jnp.concatenate([valid_half, recv_mask], axis=0)
    all_spec, all_mask = (
        lax.all_gather(local_spec, "grp", axis=0, tiled=True),
        lax.all_gather(local_mask, "grp", axis=0, tiled=True),
    )
    cross_spec = stacked(own_spec, valid_half, all_spec, all_mask)
    columns = cross_spec.shape[1]
    basis = lag_basis()
    basis_high = basis.astype(jnp.bfloat16)
    basis_low = (basis - basis_high.astype(jnp.float32)).astype(jnp.bfloat16)
    flat_cross = cross_spec.reshape(per_device * columns, 2 * NBIN)
    series = jnp.dot(flat_cross, basis_high, preferred_element_type=jnp.float32)
    series = series + jnp.dot(flat_cross, basis_low, preferred_element_type=jnp.float32)
    series = series.reshape(per_device, columns, -1)
    scaled = series * (pair_mask.astype(jnp.float32) / math.sqrt(NBIN))[:, :, None]
    return scaled.astype(jnp.bfloat16)


def solution(mesh):
    return jax.shard_map(
        on_device,
        mesh=mesh,
        in_specs=(
            P(("tile", "grp"), None, None),
            P(("tile", "grp"), None),
            P(("tile", "grp"), None, None),
            P(("tile", "grp"), None),
            P(("tile", "grp"), None),
        ),
        out_specs=P(("tile", "grp"), None, None),
        check_vma=False,
    )
```

profile of v0, /device:TPU:184, one launch (start us, length us, event | category | flops | bytes accessed | tf_op | source)
XLA Modules:
  0.0 117.1 jit_solution(16800844627624242405)
XLA Ops:
  0.0 0.0 copy-start.4
  0.0 1.3 %fusion.42 = (s32[1,1]{1,0:T(1,128)}, s32[1,1]{1,0:T(1,128)}) fusion(s32[1,2]{1,0:T(1,128)} %param.12), kind=kLoop, calls=%fused_computation.103 | loop fusion | bytes 16 | tf_op jit(solution)/shard_map/slice | solution.py:83
  1.3 1.4 %compare_and_fusion.1 = (pred[4]{0:T(512)(128)(4,1)S(1)}, s32[4]{0:T(128)S(1)}, pred[4]{0:T(512)(128)(4,1)S(1)}, s32[4]{0:T(128)S(1)}, f32[4]{0:T(128)S(1)}) fusion(s32[1,2,4]{2,1,0:T(2,128)} %param.11, s32[]{:T(128)} %bitcast.12), kind=kLoop, calls=%fused_computation.90 | loop fusion | flops 56 | bytes 92 | tf_op jit(solution)/shard_map/jit(_take)/and | solution.py:89
  2.7 0.0 copy-start.5
  2.8 1.6 %gather_fusion.1 = f32[4,16,1500]{2,1,0:T(8,128)S(1)} fusion(f32[4,16,1500]{2,1,0:T(8,128)} %param.9, s32[1024]{0:T(1024)S(1)} %pad_clamp_fusion), kind=kCustom, calls=%fused_computation.2.clone | custom fusion | bytes 768016 | tf_op jit(solution)/shard_map/jit(_take)/gather | solution.py:97
  4.3 0.1 select_multiply_fusion
  4.4 4.1 %collective-permute-start.1 = (f32[4,16,1500]{2,1,0:T(8,128)S(1)}, f32[4,16,1500]{2,1,0:T(8,128)S(1)}, u32[]{:S(2)}, u32[]{:S(2)}) collective-permute-start(f32[4,16,1500]{2,1,0:T(8,128)S(1)} %select_multiply_fusion), channel_id=1, source_target_pairs={{8,0},{16,8},{24,16},{32,24},{40,32},{48,40},{56,48},{64,56},{72,6... | collective-permute-start | bytes 1152008 | tf_op jit(solution)/shard_map/ppermute | solution.py:16
  8.6 0.0 copy-done.4
  8.6 0.6 gather_fusion
  9.2 0.7 compare_convert_fusion.1
  9.8 0.1 select_multiply_fusion.1
  9.9 1.9 %collective-permute-start = (f32[4,16,1500]{2,1,0:T(8,128)S(1)}, f32[4,16,1500]{2,1,0:T(8,128)}, u32[]{:S(2)}, u32[]{:S(2)}) collective-permute-start(f32[4,16,1500]{2,1,0:T(8,128)S(1)} %select_multiply_fusion.1), channel_id=1, source_target_pairs={{0,8},{8,16},{16,24},{24,32},{32,40},{40,48},{48,56},{56,64},{64,7... | collective-permute-start | bytes 1152008 | tf_op jit(solution)/shard_map/ppermute | solution.py:16
  11.8 0.0 copy-done.5
  11.9 0.6 gather_fusion.3
  12.4 0.1 select_multiply_fusion.2
  12.5 7.9 %collective-permute-start.3 = (f32[4,16]{1,0:T(4,128)S(1)}, f32[4,16]{1,0:T(4,128)S(1)}, u32[]{:S(2)}, u32[]{:S(2)}) collective-permute-start(f32[4,16]{1,0:T(4,128)S(1)} %select_multiply_fusion.2), channel_id=1, source_target_pairs={{8,0},{16,8},{24,16},{32,24},{40,32},{48,40},{56,48},{64,56},{72,6... | collective-permute-start | bytes 776 | tf_op jit(solution)/shard_map/ppermute | solution.py:16
  20.4 0.6 gather_fusion.2
  20.9 0.1 select_multiply_fusion.3
  21.0 1.9 %collective-permute-start.2 = (f32[4,16]{1,0:T(4,128)S(1)}, f32[4,16]{1,0:T(4,128)S(1)}, u32[]{:S(2)}, u32[]{:S(2)}) collective-permute-start(f32[4,16]{1,0:T(4,128)S(1)} %select_multiply_fusion.3), channel_id=1, source_target_pairs={{0,8},{8,16},{16,24},{24,32},{32,40},{40,48},{48,56},{56,64},{64,7... | collective-permute-start | bytes 776 | tf_op jit(solution)/shard_map/ppermute | solution.py:16
  22.9 0.1 multiply_subtract_fusion
  23.0 3.7 %fusion.16 = (f32[1500,144]{0,1:T(8,128)S(1)}, f32[1500,144]{0,1:T(8,128)S(1)}) fusion(s32[144]{0:T(256)S(1)} %iota_add_fusion.1), kind=kLoop, calls=%fused_computation.35 | loop fusion | flops 2160000 | bytes 1728576 | tf_op jit(solution)/shard_map/cos | solution.py:26
  26.7 0.1 pad_maximum_fusion.2
  26.8 1.9 %fusion.23 = f32[4,16,2,144]{3,1,2,0:T(8,128)S(1)} fusion(f32[2,144,1500,1]{2,1,0,3:T(8,128)S(1)} %bitcast.98, f32[4,16,1500]{2,1,0:T(8,128)S(1)} %copy-done.4, f32[1500]{0:T(1024)S(1)} %multiply_subtract_fusion), kind=kOutput, calls=%fused_computation.44 | convolution fusion | flops 331872000 | bytes 2191728 | tf_op jit(solution)/shard_map/dot_general | solution.py:42
  28.7 0.0 copy-start.6
  28.7 0.1 fusion.39
  28.8 0.2 multiply_convert_fusion.4
  29.1 6.1 %fusion.9 = (f32[144,2001]{1,0:T(8,128)}, f32[144,2001]{1,0:T(8,128)}) fusion(s32[2001]{0:T(1024)S(1)} %iota_add_fusion, s32[144]{0:T(256)S(1)} %iota_add_fusion.1), kind=kLoop, calls=%fused_computation.25 | loop fusion | flops 2881440 | bytes 2313732 | tf_op jit(solution)/shard_map/cos | solution.py:34
  35.2 0.0 copy-done.6
  35.2 0.2 copy.27
  35.4 0.0 collective-permute-done.3
  35.4 0.0 collective-permute-done.2
  35.4 28.1 %all-gather = bf16[8,12,16]{2,1,0:T(8,128)(2,1)S(1)} all-gather(bf16[1,12,16]{2,1,0:T(8,128)(2,1)S(1)} %maximum_bitcast_fusion.3), channel_id=1, replica_groups=mesh['tile'=32,'grp'=8] {'grp'}, dimensions={0}, use_global_device_ids=true | all-gather | bytes 3456 | tf_op jit(solution)/shard_map/all_gather | solution.py:112
  63.5 0.1 fusion.11
  63.6 0.0 collective-permute-done.1
  63.7 0.0 collective-permute-done
  63.7 2.7 %fusion.19 = f32[8,16,2,144]{3,1,2,0:T(8,128)S(1)} fusion(f32[2,144,1500,1]{2,1,0,3:T(8,128)S(1)} %bitcast.99, f32[4,16,1500]{2,1,0:T(8,128)S(1)} %collective-permute-done.1, f32[4,16,1500]{2,1,0:T(8,128)} %collective-permute-done, f32[1500]{0:T(1024)S(1)} %multiply_subtract_fusion), kind=kOutput, calls=%fused_computation.41 | convolution fusion | flops 663936000 | bytes 2649456 | tf_op jit(solution)/shard_map/dot_general | solution.py:42
  66.3 0.1 fusion.40
  66.4 0.4 fusion.30
  66.9 31.8 %all_gather.6 = bf16[96,16,2,144]{3,1,0,2:T(8,128)(2,1)S(1)} all-gather(bf16[12,16,2,144]{3,1,0,2:T(8,128)(2,1)S(1)} %maximum_maximum_fusion), channel_id=1, replica_groups=mesh['tile'=32,'grp'=8] {'grp'}, dimensions={0}, use_global_device_ids=true | all-gather | bytes 995328 | tf_op jit(solution)/shard_map/all_gather | solution.py:111
  98.7 0.1 slice_bitcast_fusion
  98.8 0.1 fusion.38
  98.9 0.7 maximum_bitcast_fusion
  99.6 0.6 pad_maximum_fusion
  100.2 5.5 %copy.20 = bf16[96,2,32,144]{0,2,1,3:T(8,128)(2,1)} copy(bf16[96,2,32,144]{3,2,0,1:T(8,128)(2,1)S(1)} %pad_maximum_fusion) | data formatting | bytes 3538944 | tf_op jit(solution)/shard_map/stack | solution.py:63
  105.7 0.0 copy-start
  105.7 0.0 copy-start.2
  105.7 2.3 %fusion.4 = bf16[4,96,2,144]{1,0,2,3:T(4,128)(2,1)S(1)} fusion(bf16[96,2,32,144]{0,2,1,3:T(8,128)(2,1)} %copy.20, bf16[4,32,144,1]{1,0,3,2:T(4,128)(2,1)S(1)} %copy.27, f32[4,96]{1,0:T(4,128)S(1)} %fusion.11), kind=kOutput, calls=%fused_computation.18 | convolution fusion | flops 7299072 | bytes 2029056 | tf_op jit(solution)/shard_map/iqf,jcqf->ijcf/dot_general | solution.py:70
  108.0 0.1 copy.23
  108.1 0.2 reshape.85
  108.3 0.0 copy-done
  108.3 0.0 copy-done.2
  108.3 0.0 copy-start.1
  108.3 0.0 copy-start.3
  108.3 1.3 %fusion.1 = f32[384,2001]{0,1:T(8,128)S(1)} fusion(bf16[384,288]{0,1:T(8,128)(2,1)S(1)} %reshape.85, f32[144,2001]{1,0:T(8,128)S(1)} %copy-done.2, f32[144,2001]{1,0:T(8,128)S(1)} %copy-done), kind=kOutput, calls=%fused_computation.14 | convolution fusion | flops 444894336 | bytes 5599872 | tf_op jit(solution)/shard_map/dot_general | solution.py:120
  109.6 0.0 copy-done.1
  109.6 0.3 copy-done.3
  109.9 1.3 %convolution_add_fusion = f32[384,2001]{0,1:T(8,128)S(1)} fusion(f32[384,2001]{0,1:T(8,128)S(1)} %fusion.1, bf16[384,288]{0,1:T(8,128)(2,1)S(1)} %reshape.85, f32[144,2001]{1,0:T(8,128)S(1)} %copy-done.3, f32[144,2001]{1,0:T(8,128)S(1)} %copy-done.1), kind=kOutput, calls=%fused_computation.6 | convolution fusion | flops 446239008 | bytes 8673408 | tf_op jit(solution)/shard_map/dot_general | solution.py:121
  111.3 2.6 %copy.24 = f32[384,2001]{1,0:T(8,128)} copy(f32[384,2001]{0,1:T(8,128)S(1)} %convolution_add_fusion) | data formatting | bytes 6147072 | tf_op jit(solution)/shard_map/add | solution.py:121
  113.8 3.3 %multiply_convert_fusion = bf16[4,96,2001]{2,1,0:T(8,128)(2,1)} fusion(f32[4,96,2001]{2,1,0:T(8,128)} %bitcast.100, f32[4,96]{1,0:T(4,128)S(1)} %convert_multiply_fusion), kind=kLoop, calls=%fused_computation.5 | loop fusion | flops 1536768 | bytes 4611840 | tf_op jit(solution)/shard_map/convert_element_type | solution.py:124
  (16 shorter events, 0.2 us)
Async XLA Ops:
  0.0 8.6 %copy-start.4 = (f32[4,16,1500]{2,1,0:T(8,128)S(1)}, f32[4,16,1500]{2,1,0:T(8,128)}, u32[]{:S(2)}) copy-start(f32[4,16,1500]{2,1,0:T(8,128)} %param.9) | copy-start | bytes 1152004
  2.7 9.1 %copy-start.5 = (s32[4,16]{1,0:T(4,128)S(1)}, s32[4,16]{1,0:T(4,128)}, u32[]{:S(2)}) copy-start(s32[4,16]{1,0:T(4,128)} %param.10) | copy-start | bytes 772
  4.4 59.2 %collective-permute-start.1 = (f32[4,16,1500]{2,1,0:T(8,128)S(1)}, f32[4,16,1500]{2,1,0:T(8,128)S(1)}, u32[]{:S(2)}, u32[]{:S(2)}) collective-permute-start(f32[4,16,1500]{2,1,0:T(8,128)S(1)} %select_multiply_fusion), channel_id=1, source_target_pairs={{8,0},{16,8},{24,16},{32,24},{40,32},{48,40},{56,48},{64,56},{72,6... | collective-permute-start | bytes 1152008 | tf_op jit(solution)/shard_map/ppermute | solution.py:16
  9.9 53.7 %collective-permute-start = (f32[4,16,1500]{2,1,0:T(8,128)S(1)}, f32[4,16,1500]{2,1,0:T(8,128)}, u32[]{:S(2)}, u32[]{:S(2)}) collective-permute-start(f32[4,16,1500]{2,1,0:T(8,128)S(1)} %select_multiply_fusion.1), channel_id=1, source_target_pairs={{0,8},{8,16},{16,24},{24,32},{32,40},{40,48},{48,56},{56,64},{64,7... | collective-permute-start | bytes 1152008 | tf_op jit(solution)/shard_map/ppermute | solution.py:16
  12.5 22.9 %collective-permute-start.3 = (f32[4,16]{1,0:T(4,128)S(1)}, f32[4,16]{1,0:T(4,128)S(1)}, u32[]{:S(2)}, u32[]{:S(2)}) collective-permute-start(f32[4,16]{1,0:T(4,128)S(1)} %select_multiply_fusion.2), channel_id=1, source_target_pairs={{8,0},{16,8},{24,16},{32,24},{40,32},{48,40},{56,48},{64,56},{72,6... | collective-permute-start | bytes 776 | tf_op jit(solution)/shard_map/ppermute | solution.py:16
  21.0 14.4 %collective-permute-start.2 = (f32[4,16]{1,0:T(4,128)S(1)}, f32[4,16]{1,0:T(4,128)S(1)}, u32[]{:S(2)}, u32[]{:S(2)}) collective-permute-start(f32[4,16]{1,0:T(4,128)S(1)} %select_multiply_fusion.3), channel_id=1, source_target_pairs={{0,8},{8,16},{16,24},{24,32},{32,40},{40,48},{48,56},{56,64},{64,7... | collective-permute-start | bytes 776 | tf_op jit(solution)/shard_map/ppermute | solution.py:16
  28.7 6.5 %copy-start.6 = (s32[4,96]{1,0:T(4,128)S(1)}, s32[4,96]{1,0:T(4,128)}, u32[]{:S(2)}) copy-start(s32[4,96]{1,0:T(4,128)} %param.13) | copy-start | bytes 4612
  105.7 2.6 %copy-start = (f32[144,2001]{1,0:T(8,128)S(1)}, f32[144,2001]{1,0:T(8,128)}, u32[]{:S(2)}) copy-start(f32[144,2001]{1,0:T(8,128)} %get-tuple-element.23) | copy-start | bytes 3457732
  105.7 2.6 %copy-start.2 = (f32[144,2001]{1,0:T(8,128)S(1)}, f32[144,2001]{1,0:T(8,128)}, u32[]{:S(2)}) copy-start(f32[144,2001]{1,0:T(8,128)} %get-tuple-element.24) | copy-start | bytes 3457732
  108.3 1.3 %copy-start.1 = (f32[144,2001]{1,0:T(8,128)S(1)}, f32[144,2001]{1,0:T(8,128)}, u32[]{:S(2)}) copy-start(f32[144,2001]{1,0:T(8,128)} %get-tuple-element.23) | copy-start | bytes 3457732
  108.3 1.6 %copy-start.3 = (f32[144,2001]{1,0:T(8,128)S(1)}, f32[144,2001]{1,0:T(8,128)}, u32[]{:S(2)}) copy-start(f32[144,2001]{1,0:T(8,128)} %get-tuple-element.24) | copy-start | bytes 3457732
where the time goes:
time: 117 us
  blocking collectives  59.9 us (51%)
  other arithmetic  17.9 us (15%)
  starting transfers between devices  15.8 us (14%)
  local copies, waits for them, and re-layouts  13.6 us (12%)
  matrix products  9.57 us (8%)
    all_gather x1, blocking collectives, on_device(): lax.all_gather(local_spec, 'grp', axis=0, tiled=True)  31.8 us
    all_gather x1, blocking collectives, on_device(): lax.all_gather(local_mask, 'grp', axis=0, tiled=True)  28.1 us
    ppermute x4, starting transfers between devices, passed_along(): return lax.ppermute(array, axis, pairs)  15.8 us
    cos x1, other arithmetic, lag_basis(): return jnp.concatenate([jnp.cos(angles), -jnp.sin(angles)], axis=0)  6.09 us
    another operation x1, local copies, waits for them, and re-layouts, stacked(): jnp.stack([jnp.concatenate([right_real, right_imag], axis=1), jnp.concate...  5.52 us
    dot_general x2, matrix products, whitened(): jnp.dot(flat_traces, fourier_table(samples), precision=lax.Precision.HIGH...  4.58 us
    cos x1, other arithmetic, fourier_table(): return jnp.concatenate([jnp.cos(angles), -jnp.sin(angles)], axis=1)  3.66 us
    convert_element_type x1, other arithmetic, on_device(): return scaled.astype(jnp.bfloat16)  3.26 us
  transfers between devices with their start and end apart: 4, of which 0 were waited for; matrix products, arithmetic and copies ran while one was open for 13% of the time, Pallas kernels for 0%

commit v1 on v0

--- a/solution.py
+++ b/solution.py
@@ -8,6 +8,11 @@
 NBIN = 144
 MAXLAG = 1000
 LAGS = 2001
+
+
+def gather_over(x, mesh_axis, along):
+    sent = jnp.stack([x] * lax.axis_size(mesh_axis))
+    return jnp.concatenate(lax.all_to_all(sent, mesh_axis, 0, 0), axis=along)
 
 
 def passed_along(array, axis, by):
@@ -108,7 +113,7 @@
     local_spec = jnp.concatenate([own_spec, recv_spec], axis=0)
     local_mask = jnp.concatenate([valid_half, recv_mask], axis=0)
     all_spec, all_mask = (
-        lax.all_gather(local_spec, "grp", axis=0, tiled=True),
+        gather_over(local_spec, "grp", 0),
         lax.all_gather(local_mask, "grp", axis=0, tiled=True),
     )
     cross_spec = stacked(own_spec, valid_half, all_spec, all_mask)

time: 117 us -> 99.8 us (0.85)
  the two profiles are of different devices: /device:TPU:184 before, /device:TPU:70 now
where the time goes in v1:
time: 99.8 us; the launch traced here: 99.3 us
  blocking collectives  36.1 us (36%)
  starting transfers between devices  19.4 us (19%)
  local copies, waits for them, and re-layouts  17.8 us (18%)
  other arithmetic  17 us (17%)
  matrix products  8.6 us (9%)
    all_gather x1, blocking collectives, on_device(): lax.all_gather(local_mask, 'grp', axis=0, tiled=True)  36.1 us
    ppermute x4, starting transfers between devices, passed_along(): return lax.ppermute(array, axis, pairs)  13.4 us
    all_to_all x1, starting transfers between devices, gather_over(): return jnp.concatenate(lax.all_to_all(sent, mesh_axis, 0, 0), axis=along)  5.95 us
    unnamed x15, local copies, waits for them, and re-layouts  5.6 us
    cos x1, other arithmetic, lag_basis(): return jnp.concatenate([jnp.cos(angles), -jnp.sin(angles)], axis=0)  4.82 us
    cos x1, other arithmetic, fourier_table(): return jnp.concatenate([jnp.cos(angles), -jnp.sin(angles)], axis=1)  3.66 us
    dot_general x2, matrix products, whitened(): jnp.dot(flat_traces, fourier_table(samples), precision=lax.Precision.HIGH...  3.58 us
    convert_element_type x1, other arithmetic, on_device(): return scaled.astype(jnp.bfloat16)  3.26 us
  transfers between devices with their start and end apart: 5, of which 0 were waited for; matrix products, arithmetic and copies ran while one was open for 15% of the time, Pallas kernels for 0%

profile of v1, /device:TPU:70, one launch (start us, length us, event | category | flops | bytes accessed | tf_op | source)
XLA Modules:
  0.0 99.3 jit_solution(11725721447590808527)
XLA Ops:
  0.0 0.0 copy-start.2
  0.0 1.3 %fusion.54 = (s32[1,1]{1,0:T(1,128)}, s32[1,1]{1,0:T(1,128)}) fusion(s32[1,2]{1,0:T(1,128)} %param.12), kind=kLoop, calls=%fused_computation.106 | loop fusion | bytes 16 | tf_op jit(solution)/shard_map/slice | solution.py:88
  1.3 1.3 %compare_and_fusion.1 = (pred[4]{0:T(512)(128)(4,1)S(1)}, s32[4]{0:T(128)S(1)}, pred[4]{0:T(512)(128)(4,1)S(1)}, s32[4]{0:T(128)S(1)}, f32[4]{0:T(128)S(1)}) fusion(s32[1,2,4]{2,1,0:T(2,128)} %param.11, s32[]{:T(128)} %bitcast.12), kind=kLoop, calls=%fused_computation.91 | loop fusion | flops 56 | bytes 92 | tf_op jit(solution)/shard_map/jit(_take)/and | solution.py:94
  2.6 0.0 copy-start.4
  2.6 1.6 %gather_fusion.1 = f32[4,16,1500]{2,1,0:T(8,128)S(1)} fusion(f32[4,16,1500]{2,1,0:T(8,128)} %param.9, s32[1024]{0:T(1024)S(1)} %pad_clamp_fusion), kind=kCustom, calls=%fused_computation.2.clone | custom fusion | bytes 768016 | tf_op jit(solution)/shard_map/jit(_take)/gather | solution.py:102
  4.2 0.1 select_multiply_fusion
  4.3 2.2 %collective-permute-start.1 = (f32[4,16,1500]{2,1,0:T(8,128)S(1)}, f32[4,16,1500]{2,1,0:T(8,128)S(1)}, u32[]{:S(2)}, u32[]{:S(2)}) collective-permute-start(f32[4,16,1500]{2,1,0:T(8,128)S(1)} %select_multiply_fusion), channel_id=1, source_target_pairs={{8,0},{16,8},{24,16},{32,24},{40,32},{48,40},{56,48},{64,56},{72,6... | collective-permute-start | bytes 1152008 | tf_op jit(solution)/shard_map/ppermute | solution.py:21
  6.5 0.0 copy-done.2
  6.5 0.6 gather_fusion
  7.1 0.7 compare_convert_fusion.1
  7.7 0.1 select_multiply_fusion.1
  7.9 2.2 %collective-permute-start = (f32[4,16,1500]{2,1,0:T(8,128)S(1)}, f32[4,16,1500]{2,1,0:T(8,128)S(1)}, u32[]{:S(2)}, u32[]{:S(2)}) collective-permute-start(f32[4,16,1500]{2,1,0:T(8,128)S(1)} %select_multiply_fusion.1), channel_id=1, source_target_pairs={{0,8},{8,16},{16,24},{24,32},{32,40},{40,48},{48,56},{56,64},{64,7... | collective-permute-start | bytes 1152008 | tf_op jit(solution)/shard_map/ppermute | solution.py:21
  10.0 0.0 copy-done.4
  10.0 0.6 gather_fusion.3
  10.6 0.1 select_multiply_fusion.2
  10.7 3.4 %collective-permute-start.3 = (f32[4,16]{1,0:T(4,128)S(1)}, f32[4,16]{1,0:T(4,128)S(1)}, u32[]{:S(2)}, u32[]{:S(2)}) collective-permute-start(f32[4,16]{1,0:T(4,128)S(1)} %select_multiply_fusion.2), channel_id=1, source_target_pairs={{8,0},{16,8},{24,16},{32,24},{40,32},{48,40},{56,48},{64,56},{72,6... | collective-permute-start | bytes 776 | tf_op jit(solution)/shard_map/ppermute | solution.py:21
  14.1 0.6 gather_fusion.2
  14.6 0.1 select_multiply_fusion.3
  14.7 5.7 %collective-permute-start.2 = (f32[4,16]{1,0:T(4,128)S(1)}, f32[4,16]{1,0:T(4,128)S(1)}, u32[]{:S(2)}, u32[]{:S(2)}) collective-permute-start(f32[4,16]{1,0:T(4,128)S(1)} %select_multiply_fusion.3), channel_id=1, source_target_pairs={{0,8},{8,16},{16,24},{24,32},{32,40},{40,48},{48,56},{56,64},{64,7... | collective-permute-start | bytes 776 | tf_op jit(solution)/shard_map/ppermute | solution.py:21
  20.4 0.1 multiply_subtract_fusion
  20.5 3.7 %fusion.21 = (f32[1500,144]{0,1:T(8,128)S(1)}, f32[1500,144]{0,1:T(8,128)S(1)}) fusion(s32[144]{0:T(256)S(1)} %iota_add_fusion.1), kind=kLoop, calls=%fused_computation.36 | loop fusion | flops 2160000 | bytes 1728576 | tf_op jit(solution)/shard_map/cos | solution.py:31
  24.1 0.1 pad_maximum_fusion.1
  24.3 1.9 %fusion.34 = f32[4,16,2,144]{3,1,2,0:T(8,128)S(1)} fusion(f32[2,144,1500,1]{2,1,0,3:T(8,128)S(1)} %bitcast.97, f32[4,16,1500]{2,1,0:T(8,128)S(1)} %copy-done.2, f32[1500]{0:T(1024)S(1)} %multiply_subtract_fusion), kind=kOutput, calls=%fused_computation.45 | convolution fusion | flops 331872000 | bytes 2191728 | tf_op jit(solution)/shard_map/dot_general | solution.py:47
  26.2 0.1 fusion.51
  26.3 0.2 multiply_convert_fusion.4
  26.6 0.0 collective-permute-done.3
  26.6 0.0 collective-permute-done.2
  26.6 0.0 collective-permute-done.1
  26.6 0.0 collective-permute-done
  26.6 1.6 %fusion.30 = f32[8,16,2,144]{3,1,2,0:T(8,128)S(1)} fusion(f32[2,144,1500,1]{2,1,0,3:T(8,128)S(1)} %bitcast.98, f32[4,16,1500]{2,1,0:T(8,128)S(1)} %collective-permute-done.1, f32[4,16,1500]{2,1,0:T(8,128)S(1)} %collective-permute-done, f32[1500]{0:T(1024)S(1)} %multiply_subtract_fusion), kind=kOutput, calls=%fused_computation.42 | convolution fusion | flops 663936000 | bytes 2649456 | tf_op jit(solution)/shard_map/dot_general | solution.py:47
  28.3 0.1 fusion.50
  28.4 0.4 fusion.41
  28.9 1.3 %stack.50 = bf16[8,12,16,2,144]{4,2,3,1,0:T(8,128)(2,1)} broadcast(bf16[12,16,2,144]{3,1,2,0:T(8,128)(2,1)S(1)} %copy.24), dimensions={1,2,3,4} | broadcast | bytes 995328 | tf_op jit(solution)/shard_map/stack | solution.py:14
  30.2 0.0 copy-start.5
  30.2 6.0 %all-to-all-start = ((bf16[8,12,16,2,144]{4,2,3,1,0:T(8,128)(2,1)}), bf16[8,12,16,2,144]{4,2,3,1,0:T(8,128)(2,1)}, u32[]{:S(2)}, u32[]{:S(2)}) async-start(bf16[8,12,16,2,144]{4,2,3,1,0:T(8,128)(2,1)} %stack.50), calls=%async_computation | async-start | bytes 3145728 | tf_op jit(solution)/shard_map/all_to_all | solution.py:15
  36.2 0.8 copy.34
  37.0 0.0 copy-done.5
  37.0 4.8 %fusion.14 = (f32[144,2001]{1,0:T(8,128)S(1)}, f32[144,2001]{1,0:T(8,128)S(1)}) fusion(s32[2001]{0:T(1024)S(1)} %iota_add_fusion, s32[144]{0:T(256)S(1)} %iota_add_fusion.1), kind=kLoop, calls=%fused_computation.26 | loop fusion | flops 2881440 | bytes 2313732 | tf_op jit(solution)/shard_map/cos | solution.py:39
  41.9 0.0 copy-start
  41.9 0.0 copy-start.1
  41.9 36.1 %all-gather = bf16[8,12,16]{2,1,0:T(8,128)(2,1)S(1)} all-gather(bf16[1,12,16]{2,1,0:T(8,128)(2,1)S(1)} %maximum_bitcast_fusion.3), channel_id=1, replica_groups=mesh['tile'=32,'grp'=8] {'grp'}, dimensions={0}, use_global_device_ids=true | all-gather | bytes 3456 | tf_op jit(solution)/shard_map/all_gather | solution.py:117
  78.0 0.1 fusion.16
  78.1 0.0 all-to-all-done
  78.2 2.7 %fusion.52 = (bf16[96,16,1,144]{3,1,2,0:T(8,128)(2,1)}, bf16[96,16,1,144]{3,1,2,0:T(8,128)(2,1)}) fusion(bf16[96,16,2,144]{3,1,2,0:T(8,128)(2,1)} %bitcast.21), kind=kLoop, calls=%fused_computation.104 | loop fusion | bytes 1769472 | tf_op jit(solution)/shard_map/slice | solution.py:67
  80.8 2.4 %copy.41 = bf16[96,16,1,144]{0,1,3,2:T(8,128)(2,1)S(1)} copy(bf16[96,16,1,144]{3,1,2,0:T(8,128)(2,1)} %get-tuple-element.19) | data formatting | bytes 884736
  83.2 0.1 bitcast_negate_fusion
  83.3 3.2 %copy.40 = bf16[96,16,1,144]{0,1,3,2:T(8,128)(2,1)} copy(bf16[96,16,1,144]{3,1,2,0:T(8,128)(2,1)} %get-tuple-element.20) | data formatting | bytes 884736
  86.5 0.0 copy-start.3
  86.5 1.7 %maximum_bitcast_fusion = (bf16[96,1,32,144]{0,2,1,3:T(8,128)(2,1)S(1)}, bf16[96,1,32,144]{0,2,1,3:T(8,128)(2,1)S(1)}) fusion(bf16[96,16,144]{0,1,2:T(8,128)(2,1)S(1)} %bitcast.100, bf16[96,16,144]{0,1,2:T(8,128)(2,1)} %bitcast.101, bf16[96,16,144]{0,1,2:T(8,128)(2,1)S(1)} %bitcast_negate_fusion), kind=kLoop, calls=%fused_computation.20 | loop fusion | flops 3538944 | bytes 3096576 | tf_op jit(solution)/shard_map/stack | solution.py:68
  88.2 0.0 copy-done.3
  88.2 0.6 fusion.26
  88.9 0.1 copy.30
  89.0 0.2 reshape.91
  89.2 0.0 copy-done
  89.2 0.0 copy-done.1
  89.2 1.3 %fusion.5 = f32[384,2001]{0,1:T(8,128)S(1)} fusion(bf16[384,288]{0,1:T(8,128)(2,1)S(1)} %reshape.91, f32[144,2001]{1,0:T(8,128)S(1)} %get-tuple-element.24, f32[144,2001]{1,0:T(8,128)S(1)} %get-tuple-element.23), kind=kOutput, calls=%fused_computation.15 | convolution fusion | flops 444894336 | bytes 5599872 | tf_op jit(solution)/shard_map/dot_general | solution.py:125
  90.5 3.0 %convolution_add_fusion = f32[384,2001]{0,1:T(8,128)S(1)} fusion(f32[384,2001]{0,1:T(8,128)S(1)} %fusion.5, bf16[384,288]{0,1:T(8,128)(2,1)S(1)} %reshape.91, f32[144,2001]{1,0:T(8,128)} %copy-done.1, f32[144,2001]{1,0:T(8,128)} %copy-done), kind=kOutput, calls=%fused_computation.5 | convolution fusion | flops 446239008 | bytes 8673408 | tf_op jit(solution)/shard_map/dot_general | solution.py:126
  93.5 2.5 %copy.31 = f32[384,2001]{1,0:T(8,128)} copy(f32[384,2001]{0,1:T(8,128)S(1)} %convolution_add_fusion) | data formatting | bytes 6147072 | tf_op jit(solution)/shard_map/add | solution.py:126
  96.0 3.3 %multiply_convert_fusion = bf16[4,96,2001]{2,1,0:T(8,128)(2,1)} fusion(f32[4,96,2001]{2,1,0:T(8,128)} %bitcast.99, f32[4,96]{1,0:T(4,128)S(1)} %convert_multiply_fusion), kind=kLoop, calls=%fused_computation.4 | loop fusion | flops 1536768 | bytes 4611840 | tf_op jit(solution)/shard_map/convert_element_type | solution.py:129
  (17 shorter events, 0.2 us)
Async XLA Ops:
  0.0 6.5 %copy-start.2 = (f32[4,16,1500]{2,1,0:T(8,128)S(1)}, f32[4,16,1500]{2,1,0:T(8,128)}, u32[]{:S(2)}) copy-start(f32[4,16,1500]{2,1,0:T(8,128)} %param.9) | copy-start | bytes 1152004
  2.6 7.4 %copy-start.4 = (s32[4,16]{1,0:T(4,128)S(1)}, s32[4,16]{1,0:T(4,128)}, u32[]{:S(2)}) copy-start(s32[4,16]{1,0:T(4,128)} %param.10) | copy-start | bytes 772
  4.3 22.3 %collective-permute-start.1 = (f32[4,16,1500]{2,1,0:T(8,128)S(1)}, f32[4,16,1500]{2,1,0:T(8,128)S(1)}, u32[]{:S(2)}, u32[]{:S(2)}) collective-permute-start(f32[4,16,1500]{2,1,0:T(8,128)S(1)} %select_multiply_fusion), channel_id=1, source_target_pairs={{8,0},{16,8},{24,16},{32,24},{40,32},{48,40},{56,48},{64,56},{72,6... | collective-permute-start | bytes 1152008 | tf_op jit(solution)/shard_map/ppermute | solution.py:21
  7.9 18.8 %collective-permute-start = (f32[4,16,1500]{2,1,0:T(8,128)S(1)}, f32[4,16,1500]{2,1,0:T(8,128)S(1)}, u32[]{:S(2)}, u32[]{:S(2)}) collective-permute-start(f32[4,16,1500]{2,1,0:T(8,128)S(1)} %select_multiply_fusion.1), channel_id=1, source_target_pairs={{0,8},{8,16},{16,24},{24,32},{32,40},{40,48},{48,56},{56,64},{64,7... | collective-permute-start | bytes 1152008 | tf_op jit(solution)/shard_map/ppermute | solution.py:21
  10.7 15.9 %collective-permute-start.3 = (f32[4,16]{1,0:T(4,128)S(1)}, f32[4,16]{1,0:T(4,128)S(1)}, u32[]{:S(2)}, u32[]{:S(2)}) collective-permute-start(f32[4,16]{1,0:T(4,128)S(1)} %select_multiply_fusion.2), channel_id=1, source_target_pairs={{8,0},{16,8},{24,16},{32,24},{40,32},{48,40},{56,48},{64,56},{72,6... | collective-permute-start | bytes 776 | tf_op jit(solution)/shard_map/ppermute | solution.py:21
  14.7 11.9 %collective-permute-start.2 = (f32[4,16]{1,0:T(4,128)S(1)}, f32[4,16]{1,0:T(4,128)S(1)}, u32[]{:S(2)}, u32[]{:S(2)}) collective-permute-start(f32[4,16]{1,0:T(4,128)S(1)} %select_multiply_fusion.3), channel_id=1, source_target_pairs={{0,8},{8,16},{16,24},{24,32},{32,40},{40,48},{48,56},{56,64},{64,7... | collective-permute-start | bytes 776 | tf_op jit(solution)/shard_map/ppermute | solution.py:21
  30.2 6.8 %copy-start.5 = (s32[4,96]{1,0:T(4,128)S(1)}, s32[4,96]{1,0:T(4,128)}, u32[]{:S(2)}) copy-start(s32[4,96]{1,0:T(4,128)} %param.13) | copy-start | bytes 4612
  30.2 47.9 %all-to-all-start = ((bf16[8,12,16,2,144]{4,2,3,1,0:T(8,128)(2,1)}), bf16[8,12,16,2,144]{4,2,3,1,0:T(8,128)(2,1)}, u32[]{:S(2)}, u32[]{:S(2)}) async-start(bf16[8,12,16,2,144]{4,2,3,1,0:T(8,128)(2,1)} %stack.50), calls=%async_computation | async-start | bytes 3145728 | tf_op jit(solution)/shard_map/all_to_all | solution.py:15
  41.9 47.3 %copy-start = (f32[144,2001]{1,0:T(8,128)}, f32[144,2001]{1,0:T(8,128)S(1)}, u32[]{:S(2)}) copy-start(f32[144,2001]{1,0:T(8,128)S(1)} %get-tuple-element.23) | copy-start | bytes 3457732
  41.9 47.3 %copy-start.1 = (f32[144,2001]{1,0:T(8,128)}, f32[144,2001]{1,0:T(8,128)S(1)}, u32[]{:S(2)}) copy-start(f32[144,2001]{1,0:T(8,128)S(1)} %get-tuple-element.24) | copy-start | bytes 3457732
  86.5 1.8 %copy-start.3 = (bf16[4,32,144,1]{1,0,3,2:T(4,128)(2,1)S(1)}, bf16[4,32,144,1]{1,0,3,2:T(4,128)(2,1)}, u32[]{:S(2)}) copy-start(bf16[4,32,144,1]{1,0,3,2:T(4,128)(2,1)} %copy.34) | copy-start | bytes 110596
